TPU v7x, 32 devices: a whole 2x2x4 slice. The times are simulated.
32 devices in a mesh: groups: 2 (over x), mix: 16 (over z, y, core).
Axes of the slice: x: 2, y: 2, z: 4, core: 2. Of those that a mesh axis runs over, the one named last changes fastest.
Arguments:
- resid_in: bfloat16 [4096, 2048], P(('groups', 'mix')), parts along dimension 0, may hold values from -40 to 40
- head_in: bfloat16 [4096, 4096], P('groups', 'mix'), parts along dimension 0, may hold values from -6 to 6
- gate_in: bfloat16 [4096, 4096], P('groups', 'mix'), parts along dimension 0, may hold values from -64 to 64
- in_basis: bfloat16 [4096, 128], P('groups'), parts along dimension 0, may hold values from -6 to 6
- out_basis: bfloat16 [4096, 128], P('groups'), parts along dimension 0, may hold values from -6 to 6
- step_size: float32 [64, 4096], P('mix', 'groups'), parts along dimension 1, may hold values from 0 to 2
- decay_rate: float32 [64], P('mix'), may hold values from 0.5 to 2
- init_state: float32 [16, 64, 64, 128], P('groups', 'mix'), parts along dimension 0, may hold values from -0.6 to 0.6
- lengths: int32 [16], P('groups'), parts along dimension 0, may hold values from 1 to 512, 2048 in all
- norm_gain: float32 [4096], replicated, may hold values from 0.1 to 1.9
- out_proj: bfloat16 [4096, 2048], P('mix'), may hold values from -0.09375 to 0.09375
- moe_gain: float32 [2048], replicated, may hold values from 0.1 to 1.9
- expert_ids: int32 [4096, 8], P(('groups', 'mix')), parts along dimension 0, may hold values from 0 to 31, as said below
- route_weight: float32 [4096, 8], P(('groups', 'mix')), parts along dimension 0, may hold values from 0.1 to 0.4
- placement: int32 [32], replicated, may hold values from 0 to 31, each once
- w_gate: bfloat16 [32, 2048, 768], P('mix'), may hold values from -0.125 to 0.125
- w_up: bfloat16 [32, 2048, 768], P('mix'), may hold values from -0.125 to 0.125
- w_down: bfloat16 [32, 768, 2048], P('mix'), may hold values from -0.21875 to 0.21875
Outputs:
- layer_out: bfloat16 [4096, 2048], P(('groups', 'mix')), parts along dimension 0
There are 2 independent parts, one for each index of `groups`. A program takes and returns all parts, laid end to end along the dimension named above; an argument that names none is the same for every part. Nothing has to cross between parts.
Inputs may be any that keep to these rules, and one draw needn't show every extreme that they name: `expert_ids`: each row names 8 different experts. Within each aligned block of 128 rows (one device's rows), 8 experts appear exactly 64 times each, 8 others 64 / 2 times each and the rest 64 / 4 times each; each of the three sets is the same in every block. `placement`: each slot once. `lengths`: requests fill the 2048 positions in order.
All inputs are finite; a program needn't handle non-finite values.
Results may differ from a plain program's by a relative error of at most 0.013.
Values may be sent and summed in bfloat16 or wider, within the bound.
No kernel may reach another device: no remote copies, remote signals or barrier semaphores. Data moves between devices by JAX's collectives and lax.ppermute only.
A program may use at most 128 MiB of HBM per device.

v0:
```python
import jax
import jax.numpy as jnp
from jax import lax
from jax.sharding import PartitionSpec as P

HEADS = 64
HEAD_DIM = 64
SPAN = 256
epsilon = 1e-05


def request_layout(lengths, tokens_total):
    request_end = jnp.cumsum(lengths)
    request_first = request_end - lengths
    position = jnp.arange(tokens_total, dtype=jnp.int32)
    segment = jnp.sum((position[None, :] >= request_end[:, None]).astype(jnp.int32), axis=0)
    member = segment[None, :] == jnp.arange(lengths.shape[0], dtype=jnp.int32)[:, None]
    first_of = jnp.sum(jnp.where(member, request_first[:, None], 0), axis=0)
    return (segment, first_of, member)


def scan_heads(
    head_values,
    head_steps,
    head_rates,
    in_basis,
    out_basis,
    state_init,
    segment,
    first_of,
    member,
    block_len,
):
    tokens_total = head_values.shape[0]
    local_heads = head_steps.shape[0]
    head_width = head_values.shape[1] // local_heads
    blocks = tokens_total // block_len
    highest = lax.Precision.HIGHEST
    log_decay = -head_steps * head_rates[:, None]
    driven = (
        head_values.reshape(tokens_total, local_heads, head_width)
        .transpose(1, 0, 2)
        .astype(jnp.float32)
    )
    driven = driven * head_steps[:, :, None]
    drive_split = driven.reshape(local_heads, blocks, block_len, head_width).transpose(1, 0, 2, 3)
    decay_split = log_decay.reshape(local_heads, blocks, block_len).transpose(1, 0, 2)

    def split_rows(array):
        return array.reshape((blocks, block_len) + array.shape[1:])

    block_first = jnp.arange(blocks, dtype=jnp.int32) * block_len
    member_blocks = member.reshape(member.shape[0], blocks, block_len).transpose(1, 0, 2)
    init_heads = state_init.transpose(1, 0, 2, 3)
    inputs = (
        drive_split,
        decay_split,
        split_rows(in_basis),
        split_rows(out_basis),
        split_rows(segment),
        split_rows(first_of),
        member_blocks,
        block_first,
    )
    offsets = jnp.arange(block_len, dtype=jnp.int32)
    causal = offsets[None, :] <= offsets[:, None]

    def advance(states_in, block_in):
        (
            drive_heads,
            decay_heads,
            basis_block,
            readout_block,
            segment_block,
            first_block,
            member_block,
            first_pos,
        ) = block_in
        basis_wide = basis_block.astype(jnp.float32)
        readout_wide = readout_block.astype(jnp.float32)
        same_seq = (segment_block[:, None] == segment_block[None, :]) & causal
        scores = jnp.dot(readout_block, basis_block.T, preferred_element_type=jnp.float32)
        carried = first_block < first_pos
        member_wide = member_block.astype(jnp.float32)

        def one_head(state_in, drive_block, decay_block, head_init):
            running = jnp.cumsum(decay_block)
            earlier = running - decay_block
            gap_values = jnp.minimum(running[:, None] - running[None, :], 0.0)
            kernel = jnp.where(same_seq, jnp.exp(gap_values), 0.0)
            output = jnp.dot(kernel * scores, drive_block, precision=highest)
            before = jnp.max(jnp.where(same_seq, earlier[None, :], -jnp.inf), axis=1)
            weight = jnp.exp(running - before)
            from_state = jnp.dot(readout_wide, state_in.T, precision=highest)
            projected = jnp.einsum("qn,rpn->rqp", readout_wide, head_init, precision=highest)
            from_init = jnp.sum(member_wide[:, :, None] * projected, axis=0)
            output = output + weight[:, None] * jnp.where(carried[:, None], from_state, from_init)
            last_weight = jnp.where(same_seq[-1], jnp.exp(running[-1] - running), 0.0)
            state_out = jnp.dot(
                (drive_block * last_weight[:, None]).T, basis_wide, precision=highest
            )
            init_last = jnp.einsum("r,rpn->pn", member_wide[:, -1], head_init, precision=highest)
            source = jnp.where(carried[-1], state_in, init_last)
            state_out = state_out + weight[-1] * source
            return (state_out, output)

        return jax.vmap(one_head)(states_in, drive_heads, decay_heads, init_heads)

    empty_state = jnp.zeros((local_heads, head_width, in_basis.shape[1]), jnp.float32)
    _, outputs = lax.scan(advance, empty_state, inputs)
    return outputs.transpose(0, 2, 1, 3).reshape(tokens_total, local_heads * head_width)


def local(
    resid_in,
    head_in,
    gate_in,
    in_basis,
    out_basis,
    step_size,
    decay_rate,
    init_state,
    lengths,
    norm_gain,
    out_proj,
    moe_gain,
    expert_ids,
    route_weight,
    placement,
    w_gate,
    w_up,
    w_down,
):
    tokens_total = head_in.shape[0]
    model_width = out_proj.shape[1]
    devices = lax.axis_size("mix")
    tok_rows = tokens_total // devices
    segment, first_of, member = request_layout(lengths, tokens_total)
    scan_out = scan_heads(
        head_in,
        step_size,
        decay_rate,
        in_basis,
        out_basis,
        init_state,
        segment,
        first_of,
        member,
        SPAN,
    )
    gated_out = scan_out * jax.nn.silu(gate_in.astype(jnp.float32))
    regrouped = lax.all_to_all(
        gated_out.astype(jnp.bfloat16), "mix", split_axis=0, concat_axis=1, tiled=True
    ).astype(gated_out.dtype)
    squares = jnp.sum(regrouped * regrouped, axis=1)
    mixed_in = (regrouped * norm_gain).astype(jnp.bfloat16)
    full_proj = lax.all_gather(out_proj, "mix", axis=0, tiled=True)
    group_terms = jnp.einsum(
        "tgc,gcd->tgd",
        mixed_in.reshape(tok_rows, devices, -1),
        full_proj.reshape(devices, -1, model_width),
        preferred_element_type=jnp.float32,
    ).astype(jnp.bfloat16)
    group_terms = lax.optimization_barrier(group_terms)
    mixer_sum = jnp.sum(group_terms.astype(jnp.float32), axis=1)
    mixer_out = mixer_sum * lax.rsqrt(squares / (HEADS * HEAD_DIM) + epsilon)[:, None]
    hidden = resid_in.astype(jnp.float32) + mixer_out
    normed = (
        hidden * lax.rsqrt(jnp.mean(hidden * hidden, axis=1, keepdims=True) + epsilon) * moe_gain
    ).astype(jnp.bfloat16)
    top_count = expert_ids.shape[1]
    flat_ids = expert_ids.reshape(-1)
    pair_count = flat_ids.shape[0]
    experts_total = placement.shape[0]
    cap_slots = 2 * pair_count // experts_total
    choose = (flat_ids[:, None] == jnp.arange(experts_total, dtype=jnp.int32)[None, :]).astype(
        jnp.int32
    )
    slot_of = jnp.sum(choose * placement[None, :], axis=1)
    slot_rank = jnp.sum(jnp.cumsum(choose, axis=0) * choose, axis=1) - 1
    buffer_index = slot_of * cap_slots + slot_rank
    owner_token = (
        jnp.full((experts_total * cap_slots,), -1, jnp.int32)
        .at[buffer_index]
        .set(jnp.arange(pair_count, dtype=jnp.int32) // top_count)
    )
    filled = owner_token >= 0
    send_rows = jnp.where(
        filled[:, None],
        jnp.take(normed, jnp.maximum(owner_token, 0), axis=0),
        jnp.zeros((), jnp.bfloat16),
    )
    send_rows = send_rows.reshape(devices, experts_total // devices, cap_slots, model_width)
    received = lax.all_to_all(send_rows, "mix", split_axis=0, concat_axis=0, tiled=True)
    gate_part = jnp.einsum("sekd,edf->sekf", received, w_gate, preferred_element_type=jnp.float32)
    up_part = jnp.einsum("sekd,edf->sekf", received, w_up, preferred_element_type=jnp.float32)
    inner_act = (jax.nn.silu(gate_part) * up_part).astype(jnp.bfloat16)
    result = jnp.einsum(
        "sekf,efd->sekd", inner_act, w_down, preferred_element_type=jnp.float32
    ).astype(jnp.bfloat16)
    returned_rows = lax.all_to_all(result, "mix", split_axis=0, concat_axis=0, tiled=True)
    back_flat = returned_rows.reshape(experts_total * cap_slots, model_width)
    picked = jnp.take(back_flat, buffer_index, axis=0).reshape(tok_rows, top_count, model_width)
    expert_sum = jnp.sum(route_weight[:, :, None] * picked.astype(jnp.float32), axis=1)
    return (hidden + expert_sum).astype(jnp.bfloat16)


def solution(mesh):
    return jax.shard_map(
        local,
        mesh=mesh,
        in_specs=(
            P(("groups", "mix"), None),
            P("groups", "mix"),
            P("groups", "mix"),
            P("groups", None),
            P("groups", None),
            P("mix", "groups"),
            P("mix"),
            P("groups", "mix", None, None),
            P("groups"),
            P(),
            P("mix", None),
            P(),
            P(("groups", "mix"), None),
            P(("groups", "mix"), None),
            P(),
            P("mix", None, None),
            P("mix", None, None),
            P("mix", None, None),
        ),
        out_specs=P(("groups", "mix"), None),
        check_vma=False,
    )
```

profile of v0, /device:TPU:15, one launch (start us, length us, event | category | flops | bytes accessed | tf_op | source)
XLA Modules:
  0.0 655.7 jit_solution(5398734231998708079)
XLA Ops:
  11.5 2.2 copy.110
  15.5 123.0 %while.13 = (s32[]{:T(128)}, f32[4,64,128]{2,1,0:T(8,128)S(1)}, f32[8,4,256,64]{2,3,1,0:T(8,128)}, f32[8,4,256,64]{2,0,3,1:T(8,128)}, s32[8,256]{1,0:T(8,128)S(1...) while((s32[]{:T(128)}, f32[4,64,128]{2,1,0:T(8,128)S(1)}, ...), condition=%wide.region_8.9_spmd.clone, body=%wide.region_3.8_spmd.clone.sunk | while | flops 1231164672 | bytes 6564249 | solution.py:110
  17.8 1.9 fusion.115
  23.2 1.8 constant_dynamic-slice_fusion.7
  25.0 2.2 fusion.116
  33.2 1.9 fusion.115
  38.6 1.8 constant_dynamic-slice_fusion.7
  40.4 2.1 fusion.116
  44.5 1.7 convolution_add_fusion.3
  48.6 1.9 fusion.115
  54.0 1.8 constant_dynamic-slice_fusion.7
  55.8 2.2 fusion.116
  64.0 1.9 fusion.115
  69.4 1.8 constant_dynamic-slice_fusion.7
  71.2 2.2 fusion.116
  75.3 1.7 convolution_add_fusion.3
  79.4 1.9 fusion.115
  84.8 1.8 constant_dynamic-slice_fusion.7
  86.6 2.2 fusion.116
  94.8 1.9 fusion.115
  100.1 1.8 constant_dynamic-slice_fusion.7
  101.9 2.1 fusion.116
  110.2 1.9 fusion.115
  115.5 1.8 constant_dynamic-slice_fusion.7
  117.3 2.1 fusion.116
  121.4 1.7 convolution_add_fusion.3
  125.5 1.9 fusion.115
  130.9 1.8 constant_dynamic-slice_fusion.7
  132.6 2.2 fusion.116
  138.5 2.9 copy.89
  143.8 1.9 fusion.62
  147.0 6.7 %all-to-all-start = ((bf16[16,128,256]{2,1,0:T(8,128)(2,1)}), bf16[16,128,256]{2,1,0:T(8,128)(2,1)S(1)}, u32[]{:S(2)}, u32[]{:S(2)}) async-start(bf16[16,128,256]{2,1,0:T(8,128)(2,1)} %bitcast.11), calls=%async_computation | async-start | bytes 2097152 | tf_op jit(solution)/shard_map/all_to_all | solution.py:152
  154.1 9.0 %reduce-window.26 = s32[32,8,128]{2,1,0:T(8,128)S(1)} reduce-window(s32[32,8,128]{2,1,0:T(8,128)S(1)} %fusion.68, s32[]{:T(128)} %constant.97.clone.1), window={size=1x1x128 pad=0_0x0_0x127_0}, to_apply=%region_12.13 | reduce-window | flops 4161536 | bytes 262148 | tf_op jit(solution)/shard_map/reduce-window.3
  163.7 4.3 scatter_custom_fusion
  168.2 10.4 %all-to-all-done = bf16[16,128,256]{2,1,0:T(8,128)(2,1)S(1)} async-done(((bf16[16,128,256]{2,1,0:T(8,128)(2,1)}), bf16[16,128,256]{2,1,0:T(8,128)(2,1)S(1)}, u32[]{:S(2)}, u32[]{:S(2)}) %all-to-all-start) | async-done | bytes 1048608 | tf_op jit(solution)/shard_map/all_to_all | solution.py:152
  178.9 11.4 %convert_bitcast_fusion.1 = bf16[128,16,2048]{2,0,1:T(8,128)(2,1)} fusion(bf16[16,256,2048]{2,1,0:T(8,128)(2,1)} %bitcast.224, bf16[16,128,256]{2,1,0:T(8,128)(2,1)S(1)} %all-to-all-done, f32[16,256]{1,0:T(8,128)S(1)} %mul.163), kind=kOutput, calls=%fused_computation.66 | convolution fusion | flops 2153250816 | bytes 26230784 | tf_op jit(solution)/shard_map/tgc,gcd->tgd/dot_general | solution.py:158
  190.3 5.3 convert_reduce_fusion
  196.3 11.0 %gather_fusion = bf16[2048,2048]{1,0:T(8,128)(2,1)} fusion(bf16[128,2048]{1,0:T(8,128)(2,1)S(1)} %multiply_convert_fusion, s32[2048]{0:T(1024)S(1)} %maximum_clamp_fusion), kind=kCustom, calls=%fused_computation | custom fusion | bytes 16785408 | tf_op jit(solution)/shard_map/jit(_take)/gather | solution.py:190
  207.3 4.6 select_select_fusion
  212.0 187.0 %all_to_all.23 = bf16[16,2,64,2048]{3,2,1,0:T(8,128)(2,1)S(1)} all-to-all(bf16[16,2,64,2048]{3,2,1,0:T(8,128)(2,1)S(1)} %select_select_fusion), channel_id=1, replica_groups=mesh['groups'=2,'mix'=16] {'mix'}, dimensions={0} | all-to-all | bytes 16777216 | tf_op jit(solution)/shard_map/all_to_all | solution.py:194
  398.9 10.6 %fusion.39 = f32[2,16,64,768]{3,2,1,0:T(8,128)} fusion(bf16[16,2,64,2048]{3,2,1,0:T(8,128)(2,1)S(1)} %all_to_all.23, bf16[2,2048,768]{2,1,0:T(8,128)(2,1)} %param.36), kind=kOutput, calls=%fused_computation.67 | convolution fusion | flops 6442450944 | bytes 20971520 | tf_op jit(solution)/shard_map/sekd,edf->sekf/dot_general | solution.py:196
  409.6 8.5 %fusion.41 = f32[2,16,64,768]{3,2,1,0:T(8,128)} fusion(bf16[16,2,64,2048]{3,2,1,0:T(8,128)(2,1)S(1)} %all_to_all.23, bf16[2,2048,768]{2,1,0:T(8,128)(2,1)S(1)} %bitcast.249), kind=kOutput, calls=%fused_computation.69 | convolution fusion | flops 6442450944 | bytes 20971520 | tf_op jit(solution)/shard_map/sekd,edf->sekf/dot_general | solution.py:195
  418.1 14.5 %convert_bitcast_fusion = bf16[16,2,64,2048]{3,2,0,1:T(8,128)(2,1)} fusion(bf16[2,768,2048]{2,1,0:T(8,128)(2,1)} %param.37, f32[2,16,64,768]{3,2,1,0:T(8,128)} %fusion.39, f32[2,16,64,768]{3,2,1,0:T(8,128)} %fusion.41), kind=kOutput, calls=%fused_computation.64 | convolution fusion | flops 6456082432 | bytes 27262976 | tf_op jit(solution)/shard_map/sekf,efd->sekd/dot_general | solution.py:198
  432.6 8.3 %copy.99 = bf16[16,2,64,2048]{3,2,1,0:T(8,128)(2,1)} copy(bf16[16,2,64,2048]{3,2,0,1:T(8,128)(2,1)} %convert_bitcast_fusion) | data formatting | bytes 16777216 | tf_op jit(solution)/shard_map/convert_element_type | solution.py:200
  440.8 5.7 all-to-all-start.2
  446.8 182.1 %all-to-all-done.2 = bf16[16,2,64,2048]{3,2,1,0:T(8,128)(2,1)} async-done(((bf16[16,2,64,2048]{3,2,1,0:T(8,128)(2,1)}), bf16[16,2,64,2048]{3,2,1,0:T(8,128)(2,1)}, u32[]{:S(2)}, u32[]{:S(2)}) %all-to-all-start.2) | async-done | bytes 8388640 | tf_op jit(solution)/shard_map/all_to_all | solution.py:201
  628.9 13.3 %gather_fusion.1 = bf16[1024,2048]{1,0:T(8,128)(2,1)} fusion(bf16[2048,2048]{1,0:T(8,128)(2,1)} %bitcast.29, s32[1024]{0:T(1024)S(1)} %broadcast_clamp_fusion), kind=kCustom, calls=%fused_computation.1 | custom fusion | bytes 8392704 | tf_op jit(solution)/shard_map/jit(_take)/gather | solution.py:203
  642.2 5.6 multiply_reduce_fusion
  (293 shorter events, 84.1 us)
Async XLA Ops:
  6.5 8.8 %copy-start.2 = (f32[4,2048]{1,0:T(4,128)S(1)}, f32[4,2048]{1,0:T(4,128)}, u32[]{:S(2)}) copy-start(f32[4,2048]{1,0:T(4,128)} %param.25) | copy-start | bytes 98308
  6.5 8.9 %copy-start.7 = (f32[4]{0:T(128)S(1)}, f32[4]{0:T(128)}, u32[]{:S(2)}) copy-start(f32[4]{0:T(128)} %param.26) | copy-start | bytes 52
  6.5 172.4 %all-gather.2.cloned.1.call-start = ((), (), s32[]{:S(2)}) async-start(), calls=%async_computation.3 | async-start | bytes 17825792 | tf_op jit(solution)/shard_map/all_gather | solution.py:157
  138.5 3.8 copy-start.1
  142.3 11.4 %copy-start.5 = (s32[128,8]{0,1:T(8,128)S(1)}, s32[128,8]{0,1:T(8,128)}, u32[]{:S(2)}) copy-start(s32[128,8]{0,1:T(8,128)} %param.32) | copy-start | bytes 12292
  142.3 11.7 %copy-start.3 = (f32[4096]{0:T(1024)S(1)}, f32[4096]{0:T(1024)}, u32[]{:S(2)}) copy-start(f32[4096]{0:T(1024)} %param.29) | copy-start | bytes 49156
  142.3 21.2 %copy-start.8 = (s32[32]{0:T(128)S(1)}, s32[32]{0:T(128)}, u32[]{:S(2)}) copy-start(s32[32]{0:T(128)} %param.34) | copy-start | bytes 388
  147.0 31.6 %all-to-all-start = ((bf16[16,128,256]{2,1,0:T(8,128)(2,1)}), bf16[16,128,256]{2,1,0:T(8,128)(2,1)S(1)}, u32[]{:S(2)}, u32[]{:S(2)}) async-start(bf16[16,128,256]{2,1,0:T(8,128)(2,1)} %bitcast.11), calls=%async_computation | async-start | bytes 2097152 | tf_op jit(solution)/shard_map/all_to_all | solution.py:152
  190.3 5.4 copy-start
  190.3 5.7 copy-start.4
  211.9 197.6 %slice-start = ((s8[6291456]{0:T(1024)(128)(4,1)}), s8[4194304]{0:T(1024)(128)(4,1)S(1)}, s32[]{:S(2)}) async-start(s8[6291456]{0:T(1024)(128)(4,1)} %bitcast.248), calls=%async_computation.4 | async-start | bytes 8388608
  398.9 10.6 %slice-start.1 = ((s8[6291456]{0:T(1024)(128)(4,1)}), s8[2097152]{0:T(1024)(128)(4,1)S(1)}, s32[]{:S(2)}) async-start(s8[6291456]{0:T(1024)(128)(4,1)} %bitcast.248), calls=%async_computation.5 | async-start | bytes 4194304
  440.8 5.8 copy-start.6
  440.8 188.1 %all-to-all-start.2 = ((bf16[16,2,64,2048]{3,2,1,0:T(8,128)(2,1)}), bf16[16,2,64,2048]{3,2,1,0:T(8,128)(2,1)}, u32[]{:S(2)}, u32[]{:S(2)}) async-start(bf16[16,2,64,2048]{3,2,1,0:T(8,128)(2,1)} %copy.99), calls=%async_computation.2 | async-start | bytes 16777216 | tf_op jit(solution)/shard_map/all_to_all | solution.py:201
Sparse Core Ops, SparseCore 0:
  9.5 125.3 all-gather.1
where the time goes:
time: 658 us; the launch traced here: 656 us
  waiting for transfers between devices  193 us (29%)
  blocking collectives  187 us (28%)
  matrix products  118 us (18%)
  local copies, waits for them, and re-layouts  79.6 us (12%)
  other arithmetic  51.1 us (8%)
  between operations  13.8 us (2%)
  starting transfers between devices  12.5 us (2%)
    all_to_all x1, blocking collectives, local(): lax.all_to_all(send_rows, 'mix', split_axis=0, concat_axis=0, tiled=True)  187 us
    all_to_all x1, waiting for transfers between devices, local(): lax.all_to_all(result, 'mix', split_axis=0, concat_axis=0, tiled=True)  182 us
    another operation x20, other arithmetic  20.1 us
    dynamic_slice x32, local copies, waits for them, and re-layouts, scan_heads(): _, outputs = lax.scan(advance, empty_state, inputs)  19.4 us
    dot_general x8, matrix products, one_head(): output = jnp.dot(kernel * scores, drive_block, precision=highest)  17.2 us
    dot_general x8, matrix products, one_head(): jnp.einsum('qn,rpn->rqp', readout_wide, head_init, precision=highest)  14.9 us
    dot_general x1, matrix products, local(): jnp.einsum('sekf,efd->sekd', inner_act, w_down, preferred_element_type=jn...  14.5 us
    dot_general x8, matrix products, one_head(): jnp.dot((drive_block * last_weight[:, None]).T, basis_wide, precision=hig...  13.8 us
  transfers between devices with their start and end apart: 3, of which 2 were waited for; matrix products, arithmetic and copies ran while one was open for 23% of the time, Pallas kernels for 0%

commit v1 on v0

--- a/solution.py
+++ b/solution.py
@@ -7,6 +7,22 @@
 HEAD_DIM = 64
 SPAN = 256
 epsilon = 1e-05
+
+
+def pairwise_exchange(array, axis, split, join):
+    ways, here = (lax.axis_size(axis), lax.axis_index(axis))
+    width = array.shape[split] // ways
+    lengths = list(array.shape)
+    lengths[split] = width
+    height = lengths[join]
+    lengths[join] = height * ways
+    full = jnp.zeros(lengths, array.dtype)
+    for mask in range(ways):
+        part = lax.dynamic_slice_in_dim(array, (here ^ mask) * width, width, axis=split)
+        if mask:
+            part = lax.ppermute(part, axis, [(d, d ^ mask) for d in range(ways)])
+        full = lax.dynamic_update_slice_in_dim(full, part, (here ^ mask) * height, axis=join)
+    return full
 
 
 def request_layout(lengths, tokens_total):
@@ -198,7 +214,7 @@
     result = jnp.einsum(
         "sekf,efd->sekd", inner_act, w_down, preferred_element_type=jnp.float32
     ).astype(jnp.bfloat16)
-    returned_rows = lax.all_to_all(result, "mix", split_axis=0, concat_axis=0, tiled=True)
+    returned_rows = pairwise_exchange(result, "mix", 0, 0)
     back_flat = returned_rows.reshape(experts_total * cap_slots, model_width)
     picked = jnp.take(back_flat, buffer_index, axis=0).reshape(tok_rows, top_count, model_width)
     expert_sum = jnp.sum(route_weight[:, :, None] * picked.astype(jnp.float32), axis=1)

time: 658 us -> 687 us (1.044)
  blocking collectives: 187 us -> 0 us
  waiting for transfers between devices: 193 us -> 365 us
  local copies, waits for them, and re-layouts: 79.6 us -> 98.4 us
  starting transfers between devices: 12.5 us -> 27.5 us
    all_to_all x1 -> x0, blocking collectives: 187 us -> none  [local(): lax.all_to_all(send_rows, 'mix', split_axis=0, concat_axis=0, tiled=True)]
    ppermute x0 -> x15, waiting for transfers between devices: none -> 172 us  [pairwise_exchange(): part = lax.ppermute(part, axis, [(d, d ^ mask) for d in range(ways)])]
    dynamic_update_slice x0 -> x16, local copies, waits for them, and re-layouts: none -> 16.7 us  [pairwise_exchange(): lax.dynamic_update_slice_in_dim(full, part, (here ^ mask) * height, axis=...]
    ppermute x0 -> x15, starting transfers between devices: none -> 15.9 us  [pairwise_exchange(): part = lax.ppermute(part, axis, [(d, d ^ mask) for d in range(ways)])]
    convert_element_type x1 -> x0, local copies, waits for them, and re-layouts: 8.25 us -> none  [local(): result = jnp.einsum('sekf,efd->sekd', inner_act, w_down, preferred_elemen...]
  transfers between devices with their start and end apart: 3 -> 18, of which waited for: 2 -> 12; matrix products, arithmetic and copies ran while one was open for 23% -> 25% of each run, Pallas kernels for 0% -> 0%
where the time goes in v1:
time: 687 us; the launch traced here: 684 us
  waiting for transfers between devices  365 us (53%)
  matrix products  124 us (18%)
  local copies, waits for them, and re-layouts  98.4 us (14%)
  other arithmetic  53.9 us (8%)
  starting transfers between devices  27.5 us (4%)
  between operations  14 us (2%)
    all_to_all x1, waiting for transfers between devices, local(): lax.all_to_all(send_rows, 'mix', split_axis=0, concat_axis=0, tiled=True)  182 us
    ppermute x15, waiting for transfers between devices, pairwise_exchange(): part = lax.ppermute(part, axis, [(d, d ^ mask) for d in range(ways)])  172 us
    another operation x20, other arithmetic  20.1 us
    dynamic_slice x32, local copies, waits for them, and re-layouts, scan_heads(): _, outputs = lax.scan(advance, empty_state, inputs)  19.4 us
    dot_general x8, matrix products, one_head(): output = jnp.dot(kernel * scores, drive_block, precision=highest)  17.2 us
    dynamic_update_slice x16, local copies, waits for them, and re-layouts, pairwise_exchange(): lax.dynamic_update_slice_in_dim(full, part, (here ^ mask) * height, axis=...  16.7 us
    ppermute x15, starting transfers between devices, pairwise_exchange(): part = lax.ppermute(part, axis, [(d, d ^ mask) for d in range(ways)])  15.9 us
    dot_general x8, matrix products, one_head(): jnp.einsum('qn,rpn->rqp', readout_wide, head_init, precision=highest)  14.9 us
  transfers between devices with their start and end apart: 18, of which 12 were waited for; matrix products, arithmetic and copies ran while one was open for 25% of the time, Pallas kernels for 0%

profile of v1, /device:TPU:15, one launch (start us, length us, event | category | flops | bytes accessed | tf_op | source)
XLA Modules:
  0.0 683.6 jit_solution(5360304544563115784)
XLA Ops:
  11.5 2.2 copy.107
  15.5 123.0 %while.13 = (s32[]{:T(128)}, f32[4,64,128]{2,1,0:T(8,128)S(1)}, f32[8,4,256,64]{2,3,1,0:T(8,128)}, f32[8,4,256,64]{2,0,3,1:T(8,128)}, s32[8,256]{1,0:T(8,128)S(1...) while((s32[]{:T(128)}, f32[4,64,128]{2,1,0:T(8,128)S(1)}, ...), condition=%wide.region_8.9_spmd.clone, body=%wide.region_3.8_spmd.clone.sunk | while | flops 1231164672 | bytes 6564249 | solution.py:126
  17.8 1.9 fusion.116
  25.0 2.2 fusion.117
  40.4 2.1 fusion.117
  48.6 1.9 fusion.116
  55.8 2.2 fusion.117
  64.0 1.9 fusion.116
  71.2 2.2 fusion.117
  79.4 1.9 fusion.116
  86.6 2.2 fusion.117
  94.8 1.9 fusion.116
  101.9 2.1 fusion.117
  117.3 2.1 fusion.117
  125.5 1.9 fusion.116
  132.6 2.2 fusion.117
  138.5 2.9 copy.87
  147.0 6.7 all-to-all-start
  154.1 9.0 %reduce-window.26 = s32[32,8,128]{2,1,0:T(8,128)S(1)} reduce-window(s32[32,8,128]{2,1,0:T(8,128)S(1)} %fusion.69, s32[]{:T(128)} %constant.66.clone.1), window={size=1x1x128 pad=0_0x0_0x127_0}, to_apply=%region_12.13 | reduce-window | flops 4161536 | bytes 262148 | tf_op jit(solution)/shard_map/reduce-window.3
  163.7 4.3 scatter_custom_fusion
  168.2 10.4 %all-to-all-done = bf16[16,128,256]{2,1,0:T(8,128)(2,1)S(1)} async-done(((bf16[16,128,256]{2,1,0:T(8,128)(2,1)}), bf16[16,128,256]{2,1,0:T(8,128)(2,1)S(1)}, u32[]{:S(2)}, u32[]{:S(2)}) %all-to-all-start) | async-done | bytes 1048608 | tf_op jit(solution)/shard_map/all_to_all | solution.py:168
  178.9 11.4 %convert_bitcast_fusion = bf16[128,16,2048]{2,0,1:T(8,128)(2,1)} fusion(bf16[16,256,2048]{2,1,0:T(8,128)(2,1)} %bitcast.254, bf16[16,128,256]{2,1,0:T(8,128)(2,1)S(1)} %all-to-all-done, f32[16,256]{1,0:T(8,128)S(1)} %mul.163), kind=kOutput, calls=%fused_computation.65 | convolution fusion | flops 2153250816 | bytes 26230784 | tf_op jit(solution)/shard_map/tgc,gcd->tgd/dot_general | solution.py:174
  190.3 5.3 convert_reduce_fusion
  196.3 11.0 %gather_fusion = bf16[2048,2048]{1,0:T(8,128)(2,1)} fusion(bf16[128,2048]{1,0:T(8,128)(2,1)S(1)} %multiply_convert_fusion, s32[2048]{0:T(1024)S(1)} %maximum_clamp_fusion), kind=kCustom, calls=%fused_computation | custom fusion | bytes 16785408 | tf_op jit(solution)/shard_map/jit(_take)/gather | solution.py:206
  207.3 7.4 %select_select_fusion = bf16[16,2,64,2048]{3,2,1,0:T(8,128)(2,1)} fusion(bf16[16,2,64,2048]{3,2,1,0:T(8,128)(2,1)} %bitcast.255, pred[16,2,64]{2,1,0:T(4,128)(4,1)S(1)} %broadcast_in_dim.139, pred[16,2,64]{2,1,0:T(4,128)(4,1)S(1)} %broadcast_in_dim.137), kind=kLoop, calls=%fused_computation.64 | loop fusion | flops 8388608 | bytes 16781312 | tf_op jit(solution)/shard_map/jit(_where)/select_n | solution.py:204
  214.7 4.9 all-to-all-start.1
  219.8 182.1 %all-to-all-done.1 = bf16[16,2,64,2048]{3,2,1,0:T(8,128)(2,1)} async-done(((bf16[16,2,64,2048]{3,2,1,0:T(8,128)(2,1)}), bf16[16,2,64,2048]{3,2,1,0:T(8,128)(2,1)}, u32[]{:S(2)}, u32[]{:S(2)}) %all-to-all-start.1) | async-done | bytes 8388640 | tf_op jit(solution)/shard_map/all_to_all | solution.py:210
  401.9 12.7 %fusion.39 = f32[2,16,64,768]{3,2,1,0:T(8,128)} fusion(bf16[16,2,64,2048]{3,2,1,0:T(8,128)(2,1)} %all-to-all-done.1, bf16[2,2048,768]{2,1,0:T(8,128)(2,1)} %param.36), kind=kOutput, calls=%fused_computation.66 | convolution fusion | flops 6442450944 | bytes 20971520 | tf_op jit(solution)/shard_map/sekd,edf->sekf/dot_general | solution.py:212
  414.6 12.6 %fusion.41 = f32[2,16,64,768]{3,2,1,0:T(8,128)} fusion(bf16[16,2,64,2048]{3,2,1,0:T(8,128)(2,1)} %all-to-all-done.1, bf16[2,2048,768]{2,1,0:T(8,128)(2,1)} %param.35), kind=kOutput, calls=%fused_computation.68 | convolution fusion | flops 6442450944 | bytes 20971520 | tf_op jit(solution)/shard_map/sekd,edf->sekf/dot_general | solution.py:211
  427.1 14.5 %fusion.51 = bf16[2,16,64,2048]{3,2,1,0:T(8,128)(2,1)} fusion(bf16[2,768,2048]{2,1,0:T(8,128)(2,1)} %param.37, f32[2,16,64,768]{3,2,1,0:T(8,128)} %fusion.39, f32[2,16,64,768]{3,2,1,0:T(8,128)} %fusion.41), kind=kOutput, calls=%fused_computation.81 | convolution fusion | flops 6456082432 | bytes 27262976 | tf_op jit(solution)/shard_map/sekf,efd->sekd/dot_general | solution.py:214
  441.7 6.1 dynamic-slice_bitcast_fusion.1
  448.1 2.1 collective-permute-start.2
  451.7 4.3 broadcast_in_dim.135
  455.9 1.9 bitcast_dynamic-update-slice_fusion
  457.9 1.9 constant_dynamic-update-slice_fusion.13
  462.7 1.9 constant_dynamic-update-slice_fusion.12
  464.6 8.7 %collective-permute-done.2 = bf16[1,2,64,2048]{3,2,1,0:T(8,128)(2,1)S(1)} collective-permute-done((bf16[1,2,64,2048]{3,2,1,0:T(8,128)(2,1)}, bf16[1,2,64,2048]{3,2,1,0:T(8,128)(2,1)S(1)}, u32[]{:S(2)}, u32[]{:S(2)}) %collective-permute-start.2) | collective-permute-done | bytes 524320 | tf_op jit(solution)/shard_map/ppermute | solution.py:23
  479.1 28.3 %collective-permute-done.5 = bf16[1,2,64,2048]{3,2,1,0:T(8,128)(2,1)S(1)} collective-permute-done((bf16[1,2,64,2048]{3,2,1,0:T(8,128)(2,1)S(1)}, bf16[1,2,64,2048]{3,2,1,0:T(8,128)(2,1)S(1)}, u32[]{:S(2)}, u32[]{:S(2)}) %collective-permute-start.5) | collective-permute-done | bytes 524320 | tf_op jit(solution)/shard_map/ppermute | solution.py:23
  507.4 4.2 collective-permute-start.10
  512.5 6.1 collective-permute-done.6
  523.6 63.7 %collective-permute-done.9 = bf16[1,2,64,2048]{3,2,1,0:T(8,128)(2,1)S(1)} collective-permute-done((bf16[1,2,64,2048]{3,2,1,0:T(8,128)(2,1)S(1)}, bf16[1,2,64,2048]{3,2,1,0:T(8,128)(2,1)S(1)}, u32[]{:S(2)}, u32[]{:S(2)}) %collective-permute-start.9) | collective-permute-done | bytes 524320 | tf_op jit(solution)/shard_map/ppermute | solution.py:23
  589.1 20.7 %collective-permute-done.10 = bf16[1,2,64,2048]{3,2,1,0:T(8,128)(2,1)S(1)} collective-permute-done((bf16[1,2,64,2048]{3,2,1,0:T(8,128)(2,1)S(1)}, bf16[1,2,64,2048]{3,2,1,0:T(8,128)(2,1)S(1)}, u32[]{:S(2)}, u32[]{:S(2)}) %collective-permute-start.10) | collective-permute-done | bytes 524320 | tf_op jit(solution)/shard_map/ppermute | solution.py:23
  610.7 10.4 %collective-permute-done.11 = bf16[1,2,64,2048]{3,2,1,0:T(8,128)(2,1)S(1)} collective-permute-done((bf16[1,2,64,2048]{3,2,1,0:T(8,128)(2,1)S(1)}, bf16[1,2,64,2048]{3,2,1,0:T(8,128)(2,1)S(1)}, u32[]{:S(2)}, u32[]{:S(2)}) %collective-permute-start.11) | collective-permute-done | bytes 524320 | tf_op jit(solution)/shard_map/ppermute | solution.py:23
  621.9 10.6 %collective-permute-done.12 = bf16[1,2,64,2048]{3,2,1,0:T(8,128)(2,1)S(1)} collective-permute-done((bf16[1,2,64,2048]{3,2,1,0:T(8,128)(2,1)S(1)}, bf16[1,2,64,2048]{3,2,1,0:T(8,128)(2,1)S(1)}, u32[]{:S(2)}, u32[]{:S(2)}) %collective-permute-start.12) | collective-permute-done | bytes 524320 | tf_op jit(solution)/shard_map/ppermute | solution.py:23
  633.3 11.4 %collective-permute-done.13 = bf16[1,2,64,2048]{3,2,1,0:T(8,128)(2,1)S(1)} collective-permute-done((bf16[1,2,64,2048]{3,2,1,0:T(8,128)(2,1)S(1)}, bf16[1,2,64,2048]{3,2,1,0:T(8,128)(2,1)S(1)}, u32[]{:S(2)}, u32[]{:S(2)}) %collective-permute-start.13) | collective-permute-done | bytes 524320 | tf_op jit(solution)/shard_map/ppermute | solution.py:23
  645.6 10.4 %collective-permute-done.14 = bf16[1,2,64,2048]{3,2,1,0:T(8,128)(2,1)S(1)} collective-permute-done((bf16[1,2,64,2048]{3,2,1,0:T(8,128)(2,1)S(1)}, bf16[1,2,64,2048]{3,2,1,0:T(8,128)(2,1)S(1)}, u32[]{:S(2)}, u32[]{:S(2)}) %collective-permute-start.14) | collective-permute-done | bytes 524320 | tf_op jit(solution)/shard_map/ppermute | solution.py:23
  656.8 13.3 %gather_fusion.1 = bf16[1024,2048]{1,0:T(8,128)(2,1)} fusion(bf16[2048,2048]{1,0:T(8,128)(2,1)} %bitcast.44, s32[1024]{0:T(1024)S(1)} %broadcast_clamp_fusion), kind=kCustom, calls=%fused_computation.1 | custom fusion | bytes 8392704 | tf_op jit(solution)/shard_map/jit(_take)/gather | solution.py:219
  670.1 5.6 multiply_reduce_fusion
  (348 shorter events, 131.4 us)
Async XLA Ops:
  6.5 8.8 %copy-start.9 = (f32[4,2048]{1,0:T(4,128)S(1)}, f32[4,2048]{1,0:T(4,128)}, u32[]{:S(2)}) copy-start(f32[4,2048]{1,0:T(4,128)} %param.25) | copy-start | bytes 98308
  6.5 8.9 %copy-start.14 = (f32[4]{0:T(128)S(1)}, f32[4]{0:T(128)}, u32[]{:S(2)}) copy-start(f32[4]{0:T(128)} %param.26) | copy-start | bytes 52
  6.5 172.4 %all-gather.2.cloned.1.call-start = ((), (), s32[]{:S(2)}) async-start(), calls=%async_computation.2 | async-start | bytes 17825792 | tf_op jit(solution)/shard_map/all_gather | solution.py:173
  138.5 3.8 copy-start.1
  141.4 12.3 %copy-start.12 = (s32[128,8]{0,1:T(8,128)S(1)}, s32[128,8]{0,1:T(8,128)}, u32[]{:S(2)}) copy-start(s32[128,8]{0,1:T(8,128)} %param.32) | copy-start | bytes 12292
  141.4 12.6 %copy-start.10 = (f32[4096]{0:T(1024)S(1)}, f32[4096]{0:T(1024)}, u32[]{:S(2)}) copy-start(f32[4096]{0:T(1024)} %param.29) | copy-start | bytes 49156
  141.4 22.1 %copy-start.15 = (s32[32]{0:T(128)S(1)}, s32[32]{0:T(128)}, u32[]{:S(2)}) copy-start(s32[32]{0:T(128)} %param.34) | copy-start | bytes 388
  147.0 31.6 %all-to-all-start = ((bf16[16,128,256]{2,1,0:T(8,128)(2,1)}), bf16[16,128,256]{2,1,0:T(8,128)(2,1)S(1)}, u32[]{:S(2)}, u32[]{:S(2)}) async-start(bf16[16,128,256]{2,1,0:T(8,128)(2,1)} %bitcast.11), calls=%async_computation | async-start | bytes 2097152 | tf_op jit(solution)/shard_map/all_to_all | solution.py:168
  190.3 5.4 copy-start
  190.3 5.7 copy-start.11
  214.7 187.2 %all-to-all-start.1 = ((bf16[16,2,64,2048]{3,2,1,0:T(8,128)(2,1)}), bf16[16,2,64,2048]{3,2,1,0:T(8,128)(2,1)}, u32[]{:S(2)}, u32[]{:S(2)}) async-start(bf16[16,2,64,2048]{3,2,1,0:T(8,128)(2,1)} %select_select_fusion), calls=%async_computation.1 | async-start | bytes 16777216 | tf_op jit(solution)/shard_map/all_to_all | solution.py:210
  441.7 6.3 copy-start.13
  447.7 10.1 %collective-permute-start = (bf16[1,2,64,2048]{3,2,1,0:T(8,128)(2,1)}, bf16[1,2,64,2048]{3,2,1,0:T(8,128)(2,1)}, u32[]{:S(2)}, u32[]{:S(2)}) collective-permute-start(bf16[1,2,64,2048]{3,2,1,0:T(8,128)(2,1)} %get-tuple-element.208), channel_id=1, source_target_pairs={{0,1},{1,0},{2,3},{3,2},{4,5},{5,4},{6,7},{7,6},{8,9},{9,8},{10,11... | collective-permute-start | bytes 1572872 | tf_op jit(solution)/shard_map/ppermute | solution.py:23
  447.9 13.5 %collective-permute-start.1 = (bf16[1,2,64,2048]{3,2,1,0:T(8,128)(2,1)}, bf16[1,2,64,2048]{3,2,1,0:T(8,128)(2,1)}, u32[]{:S(2)}, u32[]{:S(2)}) collective-permute-start(bf16[1,2,64,2048]{3,2,1,0:T(8,128)(2,1)} %get-tuple-element.207), channel_id=1, source_target_pairs={{0,2},{1,3},{2,0},{3,1},{4,6},{5,7},{6,4},{7,5},{8,10},{9,11},{10,... | collective-permute-start | bytes 1572872 | tf_op jit(solution)/shard_map/ppermute | solution.py:23
  448.1 9.8 %copy-start.8 = (bf16[1,2,64,2048]{3,2,1,0:T(8,128)(2,1)S(1)}, bf16[1,2,64,2048]{3,2,1,0:T(8,128)(2,1)}, u32[]{:S(2)}) copy-start(bf16[1,2,64,2048]{3,2,1,0:T(8,128)(2,1)} %get-tuple-element.203) | copy-start | bytes 1572868
  448.1 13.3 %copy-start.7 = (bf16[1,2,64,2048]{3,2,1,0:T(8,128)(2,1)S(1)}, bf16[1,2,64,2048]{3,2,1,0:T(8,128)(2,1)}, u32[]{:S(2)}) copy-start(bf16[1,2,64,2048]{3,2,1,0:T(8,128)(2,1)} %get-tuple-element.202) | copy-start | bytes 1572868
  448.1 25.2 %copy-start.6 = (bf16[1,2,64,2048]{3,2,1,0:T(8,128)(2,1)S(1)}, bf16[1,2,64,2048]{3,2,1,0:T(8,128)(2,1)}, u32[]{:S(2)}) copy-start(bf16[1,2,64,2048]{3,2,1,0:T(8,128)(2,1)} %get-tuple-element.201) | copy-start | bytes 1572868
  448.1 27.2 %copy-start.5 = (bf16[1,2,64,2048]{3,2,1,0:T(8,128)(2,1)S(1)}, bf16[1,2,64,2048]{3,2,1,0:T(8,128)(2,1)}, u32[]{:S(2)}) copy-start(bf16[1,2,64,2048]{3,2,1,0:T(8,128)(2,1)} %get-tuple-element.200) | copy-start | bytes 1572868
  448.1 29.0 %copy-start.4 = (bf16[1,2,64,2048]{3,2,1,0:T(8,128)(2,1)S(1)}, bf16[1,2,64,2048]{3,2,1,0:T(8,128)(2,1)}, u32[]{:S(2)}) copy-start(bf16[1,2,64,2048]{3,2,1,0:T(8,128)(2,1)} %get-tuple-element.199) | copy-start | bytes 1572868
  448.1 59.3 %copy-start.3 = (bf16[1,2,64,2048]{3,2,1,0:T(8,128)(2,1)S(1)}, bf16[1,2,64,2048]{3,2,1,0:T(8,128)(2,1)}, u32[]{:S(2)}) copy-start(bf16[1,2,64,2048]{3,2,1,0:T(8,128)(2,1)} %get-tuple-element.198) | copy-start | bytes 1572868
  448.1 70.5 %copy-start.2 = (bf16[1,2,64,2048]{3,2,1,0:T(8,128)(2,1)S(1)}, bf16[1,2,64,2048]{3,2,1,0:T(8,128)(2,1)}, u32[]{:S(2)}) copy-start(bf16[1,2,64,2048]{3,2,1,0:T(8,128)(2,1)} %get-tuple-element.197) | copy-start | bytes 1572868
  448.1 25.2 %collective-permute-start.2 = (bf16[1,2,64,2048]{3,2,1,0:T(8,128)(2,1)}, bf16[1,2,64,2048]{3,2,1,0:T(8,128)(2,1)S(1)}, u32[]{:S(2)}, u32[]{:S(2)}) collective-permute-start(bf16[1,2,64,2048]{3,2,1,0:T(8,128)(2,1)} %get-tuple-element.206), channel_id=1, source_target_pairs={{0,3},{1,2},{2,1},{3,0},{4,7},{5,6},{6,5},{7,4},{8,11},{9,10},{10,... | collective-permute-start | bytes 1572872 | tf_op jit(solution)/shard_map/ppermute | solution.py:23
  450.2 25.1 %collective-permute-start.3 = (bf16[1,2,64,2048]{3,2,1,0:T(8,128)(2,1)}, bf16[1,2,64,2048]{3,2,1,0:T(8,128)(2,1)S(1)}, u32[]{:S(2)}, u32[]{:S(2)}) collective-permute-start(bf16[1,2,64,2048]{3,2,1,0:T(8,128)(2,1)} %get-tuple-element.205), channel_id=1, source_target_pairs={{0,4},{1,5},{2,6},{3,7},{4,0},{5,1},{6,2},{7,3},{8,12},{9,13},{10,... | collective-permute-start | bytes 1572872 | tf_op jit(solution)/shard_map/ppermute | solution.py:23
  450.2 26.9 %collective-permute-start.4 = (bf16[1,2,64,2048]{3,2,1,0:T(8,128)(2,1)}, bf16[1,2,64,2048]{3,2,1,0:T(8,128)(2,1)S(1)}, u32[]{:S(2)}, u32[]{:S(2)}) collective-permute-start(bf16[1,2,64,2048]{3,2,1,0:T(8,128)(2,1)} %get-tuple-element.204), channel_id=1, source_target_pairs={{0,5},{1,4},{2,7},{3,6},{4,1},{5,0},{6,3},{7,2},{8,13},{9,12},{10,... | collective-permute-start | bytes 1572872 | tf_op jit(solution)/shard_map/ppermute | solution.py:23
  457.8 49.5 %collective-permute-start.5 = (bf16[1,2,64,2048]{3,2,1,0:T(8,128)(2,1)S(1)}, bf16[1,2,64,2048]{3,2,1,0:T(8,128)(2,1)S(1)}, u32[]{:S(2)}, u32[]{:S(2)}) collective-permute-start(bf16[1,2,64,2048]{3,2,1,0:T(8,128)(2,1)S(1)} %copy-done.8), channel_id=1, source_target_pairs={{0,6},{1,7},{2,4},{3,5},{4,2},{5,3},{6,0},{7,1},{8,14},{9,15},{10,... | collective-permute-start | bytes 1572872 | tf_op jit(solution)/shard_map/ppermute | solution.py:23
  461.3 57.3 %collective-permute-start.6 = (bf16[1,2,64,2048]{3,2,1,0:T(8,128)(2,1)S(1)}, bf16[1,2,64,2048]{3,2,1,0:T(8,128)(2,1)S(1)}, u32[]{:S(2)}, u32[]{:S(2)}) collective-permute-start(bf16[1,2,64,2048]{3,2,1,0:T(8,128)(2,1)S(1)} %copy-done.7), channel_id=1, source_target_pairs={{0,7},{1,6},{2,5},{3,4},{4,3},{5,2},{6,1},{7,0},{8,15},{9,14},{10,... | collective-permute-start | bytes 1572872 | tf_op jit(solution)/shard_map/ppermute | solution.py:23
  473.3 46.7 %collective-permute-start.7 = (bf16[1,2,64,2048]{3,2,1,0:T(8,128)(2,1)S(1)}, bf16[1,2,64,2048]{3,2,1,0:T(8,128)(2,1)S(1)}, u32[]{:S(2)}, u32[]{:S(2)}) collective-permute-start(bf16[1,2,64,2048]{3,2,1,0:T(8,128)(2,1)S(1)} %copy-done.6), channel_id=1, source_target_pairs={{0,8},{1,9},{2,10},{3,11},{4,12},{5,13},{6,14},{7,15},{8,0},{9,1},... | collective-permute-start | bytes 1572872 | tf_op jit(solution)/shard_map/ppermute | solution.py:23
  475.3 47.0 %collective-permute-start.8 = (bf16[1,2,64,2048]{3,2,1,0:T(8,128)(2,1)S(1)}, bf16[1,2,64,2048]{3,2,1,0:T(8,128)(2,1)S(1)}, u32[]{:S(2)}, u32[]{:S(2)}) collective-permute-start(bf16[1,2,64,2048]{3,2,1,0:T(8,128)(2,1)S(1)} %copy-done.5), channel_id=1, source_target_pairs={{0,9},{1,8},{2,11},{3,10},{4,13},{5,12},{6,15},{7,14},{8,1},{9,0},... | collective-permute-start | bytes 1572872 | tf_op jit(solution)/shard_map/ppermute | solution.py:23
  477.1 110.3 %collective-permute-start.9 = (bf16[1,2,64,2048]{3,2,1,0:T(8,128)(2,1)S(1)}, bf16[1,2,64,2048]{3,2,1,0:T(8,128)(2,1)S(1)}, u32[]{:S(2)}, u32[]{:S(2)}) collective-permute-start(bf16[1,2,64,2048]{3,2,1,0:T(8,128)(2,1)S(1)} %copy-done.4), channel_id=1, source_target_pairs={{0,10},{1,11},{2,8},{3,9},{4,14},{5,15},{6,12},{7,13},{8,2},{9,3},... | collective-permute-start | bytes 1572872 | tf_op jit(solution)/shard_map/ppermute | solution.py:23
  507.4 102.5 %collective-permute-start.10 = (bf16[1,2,64,2048]{3,2,1,0:T(8,128)(2,1)S(1)}, bf16[1,2,64,2048]{3,2,1,0:T(8,128)(2,1)S(1)}, u32[]{:S(2)}, u32[]{:S(2)}) collective-permute-start(bf16[1,2,64,2048]{3,2,1,0:T(8,128)(2,1)S(1)} %copy-done.3), channel_id=1, source_target_pairs={{0,11},{1,10},{2,9},{3,8},{4,15},{5,14},{6,13},{7,12},{8,3},{9,2},... | collective-permute-start | bytes 1572872 | tf_op jit(solution)/shard_map/ppermute | solution.py:23
  518.6 102.5 %collective-permute-start.11 = (bf16[1,2,64,2048]{3,2,1,0:T(8,128)(2,1)S(1)}, bf16[1,2,64,2048]{3,2,1,0:T(8,128)(2,1)S(1)}, u32[]{:S(2)}, u32[]{:S(2)}) collective-permute-start(bf16[1,2,64,2048]{3,2,1,0:T(8,128)(2,1)S(1)} %copy-done.2), channel_id=1, source_target_pairs={{0,12},{1,13},{2,14},{3,15},{4,8},{5,9},{6,10},{7,11},{8,4},{9,5},... | collective-permute-start | bytes 1572872 | tf_op jit(solution)/shard_map/ppermute | solution.py:23
  520.0 112.5 %collective-permute-start.12 = (bf16[1,2,64,2048]{3,2,1,0:T(8,128)(2,1)S(1)}, bf16[1,2,64,2048]{3,2,1,0:T(8,128)(2,1)S(1)}, u32[]{:S(2)}, u32[]{:S(2)}) collective-permute-start(bf16[1,2,64,2048]{3,2,1,0:T(8,128)(2,1)S(1)} %get-tuple-element.196), channel_id=1, source_target_pairs={{0,13},{1,12},{2,15},{3,14},{4,9},{5,8},{6,11},{7,10},{8,5},{9,4},... | collective-permute-start | bytes 1572872 | tf_op jit(solution)/shard_map/ppermute | solution.py:23
  522.4 122.4 %collective-permute-start.13 = (bf16[1,2,64,2048]{3,2,1,0:T(8,128)(2,1)S(1)}, bf16[1,2,64,2048]{3,2,1,0:T(8,128)(2,1)S(1)}, u32[]{:S(2)}, u32[]{:S(2)}) collective-permute-start(bf16[1,2,64,2048]{3,2,1,0:T(8,128)(2,1)S(1)} %get-tuple-element.195), channel_id=1, source_target_pairs={{0,14},{1,15},{2,12},{3,13},{4,10},{5,11},{6,8},{7,9},{8,6},{9,7},... | collective-permute-start | bytes 1572872 | tf_op jit(solution)/shard_map/ppermute | solution.py:23
  587.4 68.6 %collective-permute-start.14 = (bf16[1,2,64,2048]{3,2,1,0:T(8,128)(2,1)S(1)}, bf16[1,2,64,2048]{3,2,1,0:T(8,128)(2,1)S(1)}, u32[]{:S(2)}, u32[]{:S(2)}) collective-permute-start(bf16[1,2,64,2048]{3,2,1,0:T(8,128)(2,1)S(1)} %get-tuple-element.194), channel_id=1, source_target_pairs={{0,15},{1,14},{2,13},{3,12},{4,11},{5,10},{6,9},{7,8},{8,7},{9,6},... | collective-permute-start | bytes 1572872 | tf_op jit(solution)/shard_map/ppermute | solution.py:23
Sparse Core Ops, SparseCore 0:
  9.5 125.3 all-gather.1
